TPU v7x, 128 devices: a whole 4x4x4 slice. The times are simulated.
128 devices in a mesh: row: 8 (over z_lo, x), col: 16 (over y, z_hi, core).
Axes of the slice: x: 4, y: 4, z: 4 (z_hi: 2, z_lo: 2; z = z_hi * 2 + z_lo), core: 2. Of those that a mesh axis runs over, the one named last changes fastest.
Arguments:
- positions: float32 [3, 16384, 128], P(None, ('row', 'col')), may hold values from -6 to 6
- block_links: int32 [2, 16384], replicated, may hold values from 0 to 16383, as said below
- panel_points: int32 [8, 256], replicated, may hold values from 0 to 2097151
Outputs:
- smoothed: float32 [3, 32768, 128], P(None, ('row', 'col'))
- velocity: float32 [8, 3, 256], P('row', None, 'col')
Inputs may be any that keep to these rules, and one draw needn't show every extreme that they name: block_links[0, b] is an owner device, numbered in the order of row+col; block_links[1] is a permutation of the 16384 blocks whose cycles are the loops, and all blocks of one loop have one owner. The 128 blocks of one device, b // 128, include at most 2 of any one owner, and in every draw one owner has exactly 2 blocks on every device.
All inputs are finite; a program needn't handle non-finite values.
Results may differ from a plain program's by a relative error of at most 0.0003.
Values sent between devices are 32-bit elements; how exact they have to be, the bound alone decides.
A program may use at most 128 MiB of HBM per device.

v0:
```python
import math
import jax
import jax.numpy as jnp
from jax import lax
from jax.sharding import PartitionSpec as P

SWEEPS = 2
SMOOTH_RATE = 0.25
CORE_SQUARED = 0.01


def cross_three(left_vec, right_vec):
    return jnp.stack(
        [
            left_vec[1] * right_vec[2] - left_vec[2] * right_vec[1],
            left_vec[2] * right_vec[0] - left_vec[0] * right_vec[2],
            left_vec[0] * right_vec[1] - left_vec[1] * right_vec[0],
        ]
    )


def neighbours(points, next_slot, prev_slot):
    ahead = jnp.concatenate([points[:, :, 1:], points[:, next_slot, :1]], axis=2)
    behind = jnp.concatenate([points[:, prev_slot, -1:], points[:, :, :-1]], axis=2)
    return (behind, ahead)


def smooth_loops(points, next_slot, prev_slot):
    for sweep_no in range(SWEEPS):
        behind, ahead = neighbours(points, next_slot, prev_slot)
        points = points + SMOOTH_RATE * (behind - 2.0 * points + ahead)
    return points


def panel_sums(targets, sources):
    centres = sources[:3]
    segments = sources[3:]
    inner = lax.dot_general(
        targets, centres, (((0,), (0,)), ((), ())), precision=lax.Precision.HIGHEST
    )
    squared = (
        jnp.sum(targets * targets, 0)[:, None]
        + jnp.sum(centres * centres, 0)[None, :]
        - 2.0 * inner
        + CORE_SQUARED
    )
    weights = 1.0 / (squared * jnp.sqrt(squared))
    features = jnp.concatenate([segments, cross_three(segments, centres)], 0)
    return lax.dot_general(
        weights, features, (((1,), (1,)), ((), ())), precision=lax.Precision.HIGHEST
    )


def tiled_sums(targets, piece, running, largest):
    blocks = piece.shape[1]
    block_len = piece.shape[2]
    group = max(
        [
            size_try
            for size_try in (1, 2, 4, 8, 16, 32, 64, 128)
            if blocks % size_try == 0 and size_try <= largest
        ]
    )

    def one_tile(turn, accum):
        tile = lax.dynamic_slice_in_dim(piece, turn * group, group, 1).reshape(6, group * block_len)
        return accum + panel_sums(targets, tile)

    return lax.fori_loop(0, blocks // group, one_tile, running)


def shards(positions, block_links, panel_points):
    devices = lax.axis_size(("row", "col"))
    my_index = lax.axis_index(("row", "col"))
    slots = positions.shape[1]
    block_len = positions.shape[2]
    capacity = 2 * slots // devices
    held_slots = devices * capacity
    owners = block_links[0]
    follows = block_links[1]
    blocks_all = owners.shape[0]
    counter = jnp.arange(blocks_all, dtype=jnp.int32)
    precedes = jnp.zeros_like(follows).at[follows].set(counter)
    owner_grid = owners.reshape(devices, slots)
    same_owner = owner_grid[:, :, None] == owner_grid[:, None, :]
    earlier = jnp.arange(slots)[None, :] < jnp.arange(slots)[:, None]
    ranks = jnp.sum(jnp.logical_and(same_owner, earlier[None]), axis=2).reshape(blocks_all)
    places = counter // slots * capacity + ranks
    my_owner = lax.dynamic_slice_in_dim(owners, my_index * slots, slots)
    my_rank = lax.dynamic_slice_in_dim(ranks, my_index * slots, slots)
    outgoing_slot = my_owner * capacity + my_rank
    outgoing = (
        jnp.zeros((3, held_slots, block_len), jnp.float32).at[:, outgoing_slot, :].set(positions)
    )
    arrived = lax.all_to_all(outgoing, ("row", "col"), split_axis=1, concat_axis=1, tiled=True)
    is_owned = owners == my_index
    held_ids = (
        jnp.full((held_slots,), blocks_all, jnp.int32)
        .at[jnp.where(is_owned, places, held_slots)]
        .set(counter, mode="drop")
    )
    live = held_ids < blocks_all
    safe_ids = jnp.minimum(held_ids, blocks_all - 1)
    slot_index = jnp.arange(held_slots, dtype=jnp.int32)
    next_slot = jnp.where(live, places[follows[safe_ids]], slot_index)
    prev_slot = jnp.where(live, places[precedes[safe_ids]], slot_index)
    smoothed = smooth_loops(arrived, next_slot, prev_slot)
    behind, ahead = neighbours(smoothed, next_slot, prev_slot)
    segments = ahead - smoothed
    centres = 0.5 * (ahead + smoothed)
    sources = jnp.concatenate([centres, segments], 0)
    wanted = panel_points.reshape(-1)
    wanted_block = wanted // block_len
    wanted_point = wanted % block_len
    wanted_mine = owners[wanted_block] == my_index
    picked = smoothed[:, places[wanted_block], wanted_point]
    local_targets = jnp.where(wanted_mine[None, :], picked, 0.0)
    all_targets = lax.psum(local_targets, ("row", "col"))
    panel = panel_points.shape[1]
    col_count = lax.axis_size("col")
    share = panel // col_count
    scale = 1.0 / (math.pi * math.sqrt(blocks_all * block_len))
    targets = lax.dynamic_slice_in_dim(all_targets, lax.axis_index("row") * panel, panel, 1)
    zero_sums = jnp.zeros((panel, 6), jnp.float32)
    sums = tiled_sums(targets, lax.all_gather(sources, "row", axis=1, tiled=True), zero_sums, 128)
    partial_velocity = scale * (cross_three(sums[:, :3].T, targets) - sums[:, 3:].T)
    summed = lax.psum(partial_velocity, "col")
    velocity_part = lax.dynamic_slice_in_dim(summed, lax.axis_index("col") * share, share, 1)
    return (smoothed, velocity_part[None])


def solution(mesh):
    placed = (P(None, ("row", "col"), None), P(), P())
    return jax.shard_map(
        shards,
        mesh=mesh,
        in_specs=placed,
        out_specs=(P(None, ("row", "col"), None), P("row", None, "col")),
        check_vma=False,
    )
```

profile of v0, /device:TPU:0, one launch (start us, length us, event | category | flops | bytes accessed | tf_op | source)
XLA Modules:
  0.0 976.3 jit_solution(4487103491891929501)
XLA Ops:
  15.4 12.5 %scatter_fusion = f32[3,256,128]{2,0,1:T(4,128)} fusion(f32[3,256,128]{2,0,1:T(4,128)} %broadcast_in_dim.36, s32[128]{0:T(128)S(1)} %compare_select_fusion.13, f32[128,3,128]{2,1,0:T(4,128)S(1)} %copy.77), kind=kCustom, calls=%fused_computation.12 | custom fusion | bytes 590336 | tf_op jit(solution)/shard_map/scatter | solution.py:93
  40.4 60.3 %scatter_custom_fusion.1 = s32[256]{0:T(256)S(1)} fusion(s32[16384]{0:T(1024)S(1)} %bitcast.119, s32[16384]{0:T(1024)S(1)} %iota.31, s32[]{:T(128)} %constant.150.clone.1), kind=kCustom, calls=%fused_computation.120 | custom fusion | bytes 1028 | tf_op jit(solution)/shard_map/scatter | solution.py:100
  100.8 60.5 %scatter_custom_fusion.2 = s32[16384]{0:T(1024)S(1)} fusion(s32[16384]{0:T(1024)S(1)} %bitcast.118, s32[16384]{0:T(1024)S(1)} %iota.33, s32[]{:T(128)} %constant.144.clone.1), kind=kCustom, calls=%fused_computation.79 | custom fusion | bytes 65540 | tf_op jit(solution)/shard_map/scatter | solution.py:83
  217.9 11.8 %gather_fusion.9 = s32[2048]{0:T(1024)S(1)} fusion(s32[16384]{0:T(1024)S(1)} %fusion.28, s32[2048]{0:T(1024)S(1)} %broadcast_clamp_fusion), kind=kCustom, calls=%fused_computation.9 | custom fusion | bytes 24576 | tf_op jit(solution)/shard_map/gather | solution.py:116
  242.3 20.8 %gather_fusion.10 = f32[2048,3]{1,0:T(8,128)S(1)} fusion(f32[3,256,128]{0,2,1:T(8,128)} %copy.90, s32[2048]{0:T(1024)S(1)} %bitcast.100), kind=kCustom, calls=%fused_computation.10 | custom fusion | bytes 65536 | tf_op jit(solution)/shard_map/gather | solution.py:116
  263.5 80.3 %psum.14 = f32[3,2048]{0,1:T(8,128)S(1)} all-reduce(f32[3,2048]{0,1:T(8,128)S(1)} %select_bitcast_fusion), channel_id=1, replica_groups=mesh['row'=8,'col'=16] {'row','col'}, use_global_device_ids=true, to_apply=%region_4.5 | all-reduce | flops 6144 | bytes 49152 | tf_op jit(solution)/shard_map/psum | solution.py:118
  344.3 586.7 %while.16 = (s32[]{:T(128)}, f32[256,6]{0,1:T(8,128)S(1)}, f32[256]{0:T(256)S(1)}, f32[6,2048,128]{2,1,0:T(8,128)}, f32[3,256]{1,0:T(4,128)S(1)}, /*index=5*/s32...) while((s32[]{:T(128)}, f32[256,6]{0,1:T(8,128)S(1)}, ...), condition=%wide.region_8.9_spmd.clone, body=%wide.region_6.8_spmd.clone.sunk | while | flops 478678016 | bytes 36061472 | solution.py:69
  346.8 25.7 %sqrt_multiply_fusion.2 = f32[256,16384]{0,1:T(8,128)S(1)} fusion(f32[3,256]{1,0:T(4,128)S(1)} %get-tuple-element.277, f32[16384]{0:T(1024)S(1)} %bitcast.107, f32[256]{0:T(256)S(1)} %get-tuple-element.275, f32[1,3,128,128]{3,2,1,0:T(8,128)S(1)} %get-tuple-element.240), kind=kOutput, calls=%fused_computation.15.clone.1 | convolution fusion | flops 171966464 | bytes 17043456 | tf_op jit(solution)/shard_map/while/body/eval_jaxpr/dot_general | solution.py:38
  383.4 25.7 %sqrt_multiply_fusion.2 = f32[256,16384]{0,1:T(8,128)S(1)} fusion(f32[3,256]{1,0:T(4,128)S(1)} %get-tuple-element.277, f32[16384]{0:T(1024)S(1)} %bitcast.107, f32[256]{0:T(256)S(1)} %get-tuple-element.275, f32[1,3,128,128]{3,2,1,0:T(8,128)S(1)} %get-tuple-element.240), kind=kOutput, calls=%fused_computation.15.clone.1 | convolution fusion | flops 171966464 | bytes 17043456 | tf_op jit(solution)/shard_map/while/body/eval_jaxpr/dot_general | solution.py:38
  420.1 25.7 %sqrt_multiply_fusion.2 = f32[256,16384]{0,1:T(8,128)S(1)} fusion(f32[3,256]{1,0:T(4,128)S(1)} %get-tuple-element.277, f32[16384]{0:T(1024)S(1)} %bitcast.107, f32[256]{0:T(256)S(1)} %get-tuple-element.275, f32[1,3,128,128]{3,2,1,0:T(8,128)S(1)} %get-tuple-element.240), kind=kOutput, calls=%fused_computation.15.clone.1 | convolution fusion | flops 171966464 | bytes 17043456 | tf_op jit(solution)/shard_map/while/body/eval_jaxpr/dot_general | solution.py:38
  456.8 25.7 %sqrt_multiply_fusion.2 = f32[256,16384]{0,1:T(8,128)S(1)} fusion(f32[3,256]{1,0:T(4,128)S(1)} %get-tuple-element.277, f32[16384]{0:T(1024)S(1)} %bitcast.107, f32[256]{0:T(256)S(1)} %get-tuple-element.275, f32[1,3,128,128]{3,2,1,0:T(8,128)S(1)} %get-tuple-element.240), kind=kOutput, calls=%fused_computation.15.clone.1 | convolution fusion | flops 171966464 | bytes 17043456 | tf_op jit(solution)/shard_map/while/body/eval_jaxpr/dot_general | solution.py:38
  493.4 25.7 %sqrt_multiply_fusion.2 = f32[256,16384]{0,1:T(8,128)S(1)} fusion(f32[3,256]{1,0:T(4,128)S(1)} %get-tuple-element.277, f32[16384]{0:T(1024)S(1)} %bitcast.107, f32[256]{0:T(256)S(1)} %get-tuple-element.275, f32[1,3,128,128]{3,2,1,0:T(8,128)S(1)} %get-tuple-element.240), kind=kOutput, calls=%fused_computation.15.clone.1 | convolution fusion | flops 171966464 | bytes 17043456 | tf_op jit(solution)/shard_map/while/body/eval_jaxpr/dot_general | solution.py:38
  530.1 25.7 %sqrt_multiply_fusion.2 = f32[256,16384]{0,1:T(8,128)S(1)} fusion(f32[3,256]{1,0:T(4,128)S(1)} %get-tuple-element.277, f32[16384]{0:T(1024)S(1)} %bitcast.107, f32[256]{0:T(256)S(1)} %get-tuple-element.275, f32[1,3,128,128]{3,2,1,0:T(8,128)S(1)} %get-tuple-element.240), kind=kOutput, calls=%fused_computation.15.clone.1 | convolution fusion | flops 171966464 | bytes 17043456 | tf_op jit(solution)/shard_map/while/body/eval_jaxpr/dot_general | solution.py:38
  566.7 25.7 %sqrt_multiply_fusion.2 = f32[256,16384]{0,1:T(8,128)S(1)} fusion(f32[3,256]{1,0:T(4,128)S(1)} %get-tuple-element.277, f32[16384]{0:T(1024)S(1)} %bitcast.107, f32[256]{0:T(256)S(1)} %get-tuple-element.275, f32[1,3,128,128]{3,2,1,0:T(8,128)S(1)} %get-tuple-element.240), kind=kOutput, calls=%fused_computation.15.clone.1 | convolution fusion | flops 171966464 | bytes 17043456 | tf_op jit(solution)/shard_map/while/body/eval_jaxpr/dot_general | solution.py:38
  603.4 25.7 %sqrt_multiply_fusion.2 = f32[256,16384]{0,1:T(8,128)S(1)} fusion(f32[3,256]{1,0:T(4,128)S(1)} %get-tuple-element.277, f32[16384]{0:T(1024)S(1)} %bitcast.107, f32[256]{0:T(256)S(1)} %get-tuple-element.275, f32[1,3,128,128]{3,2,1,0:T(8,128)S(1)} %get-tuple-element.240), kind=kOutput, calls=%fused_computation.15.clone.1 | convolution fusion | flops 171966464 | bytes 17043456 | tf_op jit(solution)/shard_map/while/body/eval_jaxpr/dot_general | solution.py:38
  640.0 25.7 %sqrt_multiply_fusion.2 = f32[256,16384]{0,1:T(8,128)S(1)} fusion(f32[3,256]{1,0:T(4,128)S(1)} %get-tuple-element.277, f32[16384]{0:T(1024)S(1)} %bitcast.107, f32[256]{0:T(256)S(1)} %get-tuple-element.275, f32[1,3,128,128]{3,2,1,0:T(8,128)S(1)} %get-tuple-element.240), kind=kOutput, calls=%fused_computation.15.clone.1 | convolution fusion | flops 171966464 | bytes 17043456 | tf_op jit(solution)/shard_map/while/body/eval_jaxpr/dot_general | solution.py:38
  676.7 25.7 %sqrt_multiply_fusion.2 = f32[256,16384]{0,1:T(8,128)S(1)} fusion(f32[3,256]{1,0:T(4,128)S(1)} %get-tuple-element.277, f32[16384]{0:T(1024)S(1)} %bitcast.107, f32[256]{0:T(256)S(1)} %get-tuple-element.275, f32[1,3,128,128]{3,2,1,0:T(8,128)S(1)} %get-tuple-element.240), kind=kOutput, calls=%fused_computation.15.clone.1 | convolution fusion | flops 171966464 | bytes 17043456 | tf_op jit(solution)/shard_map/while/body/eval_jaxpr/dot_general | solution.py:38
  713.4 25.7 %sqrt_multiply_fusion.2 = f32[256,16384]{0,1:T(8,128)S(1)} fusion(f32[3,256]{1,0:T(4,128)S(1)} %get-tuple-element.277, f32[16384]{0:T(1024)S(1)} %bitcast.107, f32[256]{0:T(256)S(1)} %get-tuple-element.275, f32[1,3,128,128]{3,2,1,0:T(8,128)S(1)} %get-tuple-element.240), kind=kOutput, calls=%fused_computation.15.clone.1 | convolution fusion | flops 171966464 | bytes 17043456 | tf_op jit(solution)/shard_map/while/body/eval_jaxpr/dot_general | solution.py:38
  750.0 25.7 %sqrt_multiply_fusion.2 = f32[256,16384]{0,1:T(8,128)S(1)} fusion(f32[3,256]{1,0:T(4,128)S(1)} %get-tuple-element.277, f32[16384]{0:T(1024)S(1)} %bitcast.107, f32[256]{0:T(256)S(1)} %get-tuple-element.275, f32[1,3,128,128]{3,2,1,0:T(8,128)S(1)} %get-tuple-element.240), kind=kOutput, calls=%fused_computation.15.clone.1 | convolution fusion | flops 171966464 | bytes 17043456 | tf_op jit(solution)/shard_map/while/body/eval_jaxpr/dot_general | solution.py:38
  786.7 25.7 %sqrt_multiply_fusion.2 = f32[256,16384]{0,1:T(8,128)S(1)} fusion(f32[3,256]{1,0:T(4,128)S(1)} %get-tuple-element.277, f32[16384]{0:T(1024)S(1)} %bitcast.107, f32[256]{0:T(256)S(1)} %get-tuple-element.275, f32[1,3,128,128]{3,2,1,0:T(8,128)S(1)} %get-tuple-element.240), kind=kOutput, calls=%fused_computation.15.clone.1 | convolution fusion | flops 171966464 | bytes 17043456 | tf_op jit(solution)/shard_map/while/body/eval_jaxpr/dot_general | solution.py:38
  823.3 25.7 %sqrt_multiply_fusion.2 = f32[256,16384]{0,1:T(8,128)S(1)} fusion(f32[3,256]{1,0:T(4,128)S(1)} %get-tuple-element.277, f32[16384]{0:T(1024)S(1)} %bitcast.107, f32[256]{0:T(256)S(1)} %get-tuple-element.275, f32[1,3,128,128]{3,2,1,0:T(8,128)S(1)} %get-tuple-element.240), kind=kOutput, calls=%fused_computation.15.clone.1 | convolution fusion | flops 171966464 | bytes 17043456 | tf_op jit(solution)/shard_map/while/body/eval_jaxpr/dot_general | solution.py:38
  860.0 25.7 %sqrt_multiply_fusion.2 = f32[256,16384]{0,1:T(8,128)S(1)} fusion(f32[3,256]{1,0:T(4,128)S(1)} %get-tuple-element.277, f32[16384]{0:T(1024)S(1)} %bitcast.107, f32[256]{0:T(256)S(1)} %get-tuple-element.275, f32[1,3,128,128]{3,2,1,0:T(8,128)S(1)} %get-tuple-element.240), kind=kOutput, calls=%fused_computation.15.clone.1 | convolution fusion | flops 171966464 | bytes 17043456 | tf_op jit(solution)/shard_map/while/body/eval_jaxpr/dot_general | solution.py:38
  896.7 25.7 %sqrt_multiply_fusion.2 = f32[256,16384]{0,1:T(8,128)S(1)} fusion(f32[3,256]{1,0:T(4,128)S(1)} %get-tuple-element.277, f32[16384]{0:T(1024)S(1)} %bitcast.107, f32[256]{0:T(256)S(1)} %get-tuple-element.275, f32[1,3,128,128]{3,2,1,0:T(8,128)S(1)} %get-tuple-element.240), kind=kOutput, calls=%fused_computation.15.clone.1 | convolution fusion | flops 171966464 | bytes 17043456 | tf_op jit(solution)/shard_map/while/body/eval_jaxpr/dot_general | solution.py:38
  931.7 37.0 %psum.15 = f32[3,256]{1,0:T(4,128)S(1)} all-reduce(f32[3,256]{1,0:T(4,128)S(1)} %fusion.41), channel_id=1, replica_groups=mesh['row'=8,'col'=16] {'col'}, use_global_device_ids=true, to_apply=%region_9.10 | all-reduce | flops 768 | bytes 6144 | tf_op jit(solution)/shard_map/psum | solution.py:127
  (137 shorter events, 267.6 us)
Async XLA Ops:
  27.9 140.4 %all-to-all-start = ((f32[3,256,128]{2,0,1:T(4,128)}), f32[3,256,128]{2,0,1:T(4,128)S(1)}, u32[]{:S(2)}, u32[]{:S(2)}) async-start(f32[3,256,128]{2,0,1:T(4,128)} %scatter_fusion), calls=%async_computation | async-start | bytes 1048576 | tf_op jit(solution)/shard_map/all_to_all | solution.py:95
  39.1 305.2 %all-gather.2.cloned.1.call-start = ((), (), s32[]{:S(2)}) async-start(), calls=%async_computation.1 | async-start | bytes 7077888 | tf_op jit(solution)/shard_map/all_gather | solution.py:125
  194.3 23.4 %copy-start = (s32[8,256]{1,0:T(8,128)S(1)}, s32[8,256]{1,0:T(8,128)}, u32[]{:S(2)}) copy-start(s32[8,256]{1,0:T(8,128)} %param.7) | copy-start | bytes 24580
Sparse Core Ops, SparseCore 0:
  217.9 75.4 all-gather.1
where the time goes:
time: 982 us; the launch traced here: 976 us
  matrix products  550 us (56%)
  local copies, waits for them, and re-layouts  239 us (24%)
  blocking collectives  117 us (12%)
  other arithmetic  42.8 us (4%)
  between operations  14.6 us (1%)
  starting transfers between devices  11.2 us (1%)
    dot_general x16, matrix products, panel_sums(): lax.dot_general(targets, centres, (((0,), (0,)), ((), ())), precision=lax...  410 us
    dot_general x16, matrix products, panel_sums(): lax.dot_general(weights, features, (((1,), (1,)), ((), ())), precision=la...  140 us
    psum x1, blocking collectives, shards(): all_targets = lax.psum(local_targets, ('row', 'col'))  80.3 us
    scatter x1, local copies, waits for them, and re-layouts, shards(): precedes = jnp.zeros_like(follows).at[follows].set(counter)  60.5 us
    scatter x1, local copies, waits for them, and re-layouts, shards(): held_ids = jnp.full((held_slots,), blocks_all, jnp.int32).at[jnp.where(is...  60.3 us
    psum x1, blocking collectives, shards(): summed = lax.psum(partial_velocity, 'col')  37 us
    gather x2, local copies, waits for them, and re-layouts, shards(): picked = smoothed[:, places[wanted_block], wanted_point]  32.6 us
  transfers between devices with their start and end apart: 2, of which 0 were waited for; matrix products, arithmetic and copies ran while one was open for 18% of the time, Pallas kernels for 0%

commit v1 on v0

--- a/solution.py
+++ b/solution.py
@@ -115,7 +115,12 @@
     wanted_mine = owners[wanted_block] == my_index
     picked = smoothed[:, places[wanted_block], wanted_point]
     local_targets = jnp.where(wanted_mine[None, :], picked, 0.0)
-    all_targets = lax.psum(local_targets, ("row", "col"))
+
+    def remake_bars(slab_in, link_axis, lane_axis):
+        taken_in = lax.psum(slab_in, axis_name=link_axis)
+        return lax.psum(taken_in, axis_name=lane_axis)
+
+    all_targets = remake_bars(local_targets, "row", "col")
     panel = panel_points.shape[1]
     col_count = lax.axis_size("col")
     share = panel // col_count

time: 982 us -> 1050 us (1.069)
  blocking collectives: 117 us -> 183 us
    psum x1 -> x2, blocking collectives: 80.3 us -> 150 us  [the longest x1 76.5 us: remake_bars(): return lax.psum(taken_in, axis_name=lane_axis)]
  transfers between devices with their start and end apart: 2 -> 2, of which waited for: 0 -> 0; matrix products, arithmetic and copies ran while one was open for 18% -> 17% of each run, Pallas kernels for 0% -> 0%
where the time goes in v1:
time: 1050 us; the launch traced here: 1040 us
  matrix products  551 us (52%)
  local copies, waits for them, and re-layouts  239 us (23%)
  blocking collectives  183 us (17%)
  other arithmetic  42.8 us (4%)
  between operations  14.6 us (1%)
  starting transfers between devices  11.2 us (1%)
    dot_general x16, matrix products, panel_sums(): lax.dot_general(targets, centres, (((0,), (0,)), ((), ())), precision=lax...  411 us
    dot_general x16, matrix products, panel_sums(): lax.dot_general(weights, features, (((1,), (1,)), ((), ())), precision=la...  140 us
    psum x1, blocking collectives, remake_bars(): return lax.psum(taken_in, axis_name=lane_axis)  76.5 us
    psum x1, blocking collectives, remake_bars(): taken_in = lax.psum(slab_in, axis_name=link_axis)  73.2 us
    scatter x1, local copies, waits for them, and re-layouts, shards(): precedes = jnp.zeros_like(follows).at[follows].set(counter)  60.5 us
    scatter x1, local copies, waits for them, and re-layouts, shards(): held_ids = jnp.full((held_slots,), blocks_all, jnp.int32).at[jnp.where(is...  60.3 us
    psum x1, blocking collectives, shards(): summed = lax.psum(partial_velocity, 'col')  33.2 us
    gather x2, local copies, waits for them, and re-layouts, shards(): picked = smoothed[:, places[wanted_block], wanted_point]  32.6 us
  transfers between devices with their start and end apart: 2, of which 0 were waited for; matrix products, arithmetic and copies ran while one was open for 17% of the time, Pallas kernels for 0%

profile of v1, /device:TPU:0, one launch (start us, length us, event | category | flops | bytes accessed | tf_op | source)
XLA Modules:
  0.0 1042.0 jit_solution(1483917200932947082)
XLA Ops:
  15.4 12.5 %scatter_fusion = f32[3,256,128]{2,0,1:T(4,128)} fusion(f32[3,256,128]{2,0,1:T(4,128)} %broadcast_in_dim.36, s32[128]{0:T(128)S(1)} %compare_select_fusion.13, f32[128,3,128]{2,1,0:T(4,128)S(1)} %copy.77), kind=kCustom, calls=%fused_computation.12 | custom fusion | bytes 590336 | tf_op jit(solution)/shard_map/scatter | solution.py:93
  40.4 60.3 %scatter_custom_fusion.1 = s32[256]{0:T(256)S(1)} fusion(s32[16384]{0:T(1024)S(1)} %bitcast.119, s32[16384]{0:T(1024)S(1)} %iota.31, s32[]{:T(128)} %constant.150.clone.1), kind=kCustom, calls=%fused_computation.120 | custom fusion | bytes 1028 | tf_op jit(solution)/shard_map/scatter | solution.py:100
  100.8 60.5 %scatter_custom_fusion.2 = s32[16384]{0:T(1024)S(1)} fusion(s32[16384]{0:T(1024)S(1)} %bitcast.118, s32[16384]{0:T(1024)S(1)} %iota.33, s32[]{:T(128)} %constant.144.clone.1), kind=kCustom, calls=%fused_computation.79 | custom fusion | bytes 65540 | tf_op jit(solution)/shard_map/scatter | solution.py:83
  242.3 20.8 %gather_fusion.10 = f32[2048,3]{1,0:T(8,128)S(1)} fusion(f32[3,256,128]{0,2,1:T(8,128)} %copy.90, s32[2048]{0:T(1024)S(1)} %bitcast.100), kind=kCustom, calls=%fused_computation.10 | custom fusion | bytes 65536 | tf_op jit(solution)/shard_map/gather | solution.py:116
  263.5 73.2 %psum.21 = f32[3,2048]{0,1:T(8,128)S(1)} all-reduce(f32[3,2048]{0,1:T(8,128)S(1)} %select_bitcast_fusion), channel_id=1, replica_groups=mesh['row'=8,'col'=16] {'row'}, use_global_device_ids=true, to_apply=%region_4.5 | all-reduce | flops 6144 | bytes 49152 | tf_op jit(solution)/shard_map/psum | solution.py:120
  336.6 76.5 %psum.22 = f32[3,2048]{0,1:T(8,128)S(1)} all-reduce(f32[3,2048]{0,1:T(8,128)S(1)} %psum.21), channel_id=1, replica_groups=mesh['row'=8,'col'=16] {'col'}, use_global_device_ids=true, to_apply=%region_5.6 | all-reduce | flops 6144 | bytes 49152 | tf_op jit(solution)/shard_map/psum | solution.py:121
  413.7 586.9 %while.16 = (s32[]{:T(128)}, f32[256,6]{0,1:T(8,128)S(1)}, f32[256]{0:T(256)S(1)}, f32[6,2048,128]{2,1,0:T(8,128)}, f32[3,256]{1,0:T(4,128)S(1)}, /*index=5*/s32...) while((s32[]{:T(128)}, f32[256,6]{0,1:T(8,128)S(1)}, ...), condition=%wide.region_9.10_spmd.clone, body=%wide.region_7.9_spmd.clone.sunk | while | flops 478678016 | bytes 36061472 | solution.py:69
  416.1 25.7 %sqrt_multiply_fusion.2 = f32[256,16384]{0,1:T(8,128)S(1)} fusion(f32[3,256]{1,0:T(4,128)S(1)} %get-tuple-element.277, f32[16384]{0:T(1024)S(1)} %bitcast.107, f32[256]{0:T(256)S(1)} %get-tuple-element.275, f32[1,3,128,128]{3,2,1,0:T(8,128)S(1)} %get-tuple-element.240), kind=kOutput, calls=%fused_computation.15.clone.1 | convolution fusion | flops 171966464 | bytes 17043456 | tf_op jit(solution)/shard_map/while/body/eval_jaxpr/dot_general | solution.py:38
  452.8 25.7 %sqrt_multiply_fusion.2 = f32[256,16384]{0,1:T(8,128)S(1)} fusion(f32[3,256]{1,0:T(4,128)S(1)} %get-tuple-element.277, f32[16384]{0:T(1024)S(1)} %bitcast.107, f32[256]{0:T(256)S(1)} %get-tuple-element.275, f32[1,3,128,128]{3,2,1,0:T(8,128)S(1)} %get-tuple-element.240), kind=kOutput, calls=%fused_computation.15.clone.1 | convolution fusion | flops 171966464 | bytes 17043456 | tf_op jit(solution)/shard_map/while/body/eval_jaxpr/dot_general | solution.py:38
  489.5 25.7 %sqrt_multiply_fusion.2 = f32[256,16384]{0,1:T(8,128)S(1)} fusion(f32[3,256]{1,0:T(4,128)S(1)} %get-tuple-element.277, f32[16384]{0:T(1024)S(1)} %bitcast.107, f32[256]{0:T(256)S(1)} %get-tuple-element.275, f32[1,3,128,128]{3,2,1,0:T(8,128)S(1)} %get-tuple-element.240), kind=kOutput, calls=%fused_computation.15.clone.1 | convolution fusion | flops 171966464 | bytes 17043456 | tf_op jit(solution)/shard_map/while/body/eval_jaxpr/dot_general | solution.py:38
  526.2 25.7 %sqrt_multiply_fusion.2 = f32[256,16384]{0,1:T(8,128)S(1)} fusion(f32[3,256]{1,0:T(4,128)S(1)} %get-tuple-element.277, f32[16384]{0:T(1024)S(1)} %bitcast.107, f32[256]{0:T(256)S(1)} %get-tuple-element.275, f32[1,3,128,128]{3,2,1,0:T(8,128)S(1)} %get-tuple-element.240), kind=kOutput, calls=%fused_computation.15.clone.1 | convolution fusion | flops 171966464 | bytes 17043456 | tf_op jit(solution)/shard_map/while/body/eval_jaxpr/dot_general | solution.py:38
  562.8 25.7 %sqrt_multiply_fusion.2 = f32[256,16384]{0,1:T(8,128)S(1)} fusion(f32[3,256]{1,0:T(4,128)S(1)} %get-tuple-element.277, f32[16384]{0:T(1024)S(1)} %bitcast.107, f32[256]{0:T(256)S(1)} %get-tuple-element.275, f32[1,3,128,128]{3,2,1,0:T(8,128)S(1)} %get-tuple-element.240), kind=kOutput, calls=%fused_computation.15.clone.1 | convolution fusion | flops 171966464 | bytes 17043456 | tf_op jit(solution)/shard_map/while/body/eval_jaxpr/dot_general | solution.py:38
  599.5 25.7 %sqrt_multiply_fusion.2 = f32[256,16384]{0,1:T(8,128)S(1)} fusion(f32[3,256]{1,0:T(4,128)S(1)} %get-tuple-element.277, f32[16384]{0:T(1024)S(1)} %bitcast.107, f32[256]{0:T(256)S(1)} %get-tuple-element.275, f32[1,3,128,128]{3,2,1,0:T(8,128)S(1)} %get-tuple-element.240), kind=kOutput, calls=%fused_computation.15.clone.1 | convolution fusion | flops 171966464 | bytes 17043456 | tf_op jit(solution)/shard_map/while/body/eval_jaxpr/dot_general | solution.py:38
  636.2 25.7 %sqrt_multiply_fusion.2 = f32[256,16384]{0,1:T(8,128)S(1)} fusion(f32[3,256]{1,0:T(4,128)S(1)} %get-tuple-element.277, f32[16384]{0:T(1024)S(1)} %bitcast.107, f32[256]{0:T(256)S(1)} %get-tuple-element.275, f32[1,3,128,128]{3,2,1,0:T(8,128)S(1)} %get-tuple-element.240), kind=kOutput, calls=%fused_computation.15.clone.1 | convolution fusion | flops 171966464 | bytes 17043456 | tf_op jit(solution)/shard_map/while/body/eval_jaxpr/dot_general | solution.py:38
  672.8 25.7 %sqrt_multiply_fusion.2 = f32[256,16384]{0,1:T(8,128)S(1)} fusion(f32[3,256]{1,0:T(4,128)S(1)} %get-tuple-element.277, f32[16384]{0:T(1024)S(1)} %bitcast.107, f32[256]{0:T(256)S(1)} %get-tuple-element.275, f32[1,3,128,128]{3,2,1,0:T(8,128)S(1)} %get-tuple-element.240), kind=kOutput, calls=%fused_computation.15.clone.1 | convolution fusion | flops 171966464 | bytes 17043456 | tf_op jit(solution)/shard_map/while/body/eval_jaxpr/dot_general | solution.py:38
  709.5 25.7 %sqrt_multiply_fusion.2 = f32[256,16384]{0,1:T(8,128)S(1)} fusion(f32[3,256]{1,0:T(4,128)S(1)} %get-tuple-element.277, f32[16384]{0:T(1024)S(1)} %bitcast.107, f32[256]{0:T(256)S(1)} %get-tuple-element.275, f32[1,3,128,128]{3,2,1,0:T(8,128)S(1)} %get-tuple-element.240), kind=kOutput, calls=%fused_computation.15.clone.1 | convolution fusion | flops 171966464 | bytes 17043456 | tf_op jit(solution)/shard_map/while/body/eval_jaxpr/dot_general | solution.py:38
  746.2 25.7 %sqrt_multiply_fusion.2 = f32[256,16384]{0,1:T(8,128)S(1)} fusion(f32[3,256]{1,0:T(4,128)S(1)} %get-tuple-element.277, f32[16384]{0:T(1024)S(1)} %bitcast.107, f32[256]{0:T(256)S(1)} %get-tuple-element.275, f32[1,3,128,128]{3,2,1,0:T(8,128)S(1)} %get-tuple-element.240), kind=kOutput, calls=%fused_computation.15.clone.1 | convolution fusion | flops 171966464 | bytes 17043456 | tf_op jit(solution)/shard_map/while/body/eval_jaxpr/dot_general | solution.py:38
  782.8 25.7 %sqrt_multiply_fusion.2 = f32[256,16384]{0,1:T(8,128)S(1)} fusion(f32[3,256]{1,0:T(4,128)S(1)} %get-tuple-element.277, f32[16384]{0:T(1024)S(1)} %bitcast.107, f32[256]{0:T(256)S(1)} %get-tuple-element.275, f32[1,3,128,128]{3,2,1,0:T(8,128)S(1)} %get-tuple-element.240), kind=kOutput, calls=%fused_computation.15.clone.1 | convolution fusion | flops 171966464 | bytes 17043456 | tf_op jit(solution)/shard_map/while/body/eval_jaxpr/dot_general | solution.py:38
  819.5 25.7 %sqrt_multiply_fusion.2 = f32[256,16384]{0,1:T(8,128)S(1)} fusion(f32[3,256]{1,0:T(4,128)S(1)} %get-tuple-element.277, f32[16384]{0:T(1024)S(1)} %bitcast.107, f32[256]{0:T(256)S(1)} %get-tuple-element.275, f32[1,3,128,128]{3,2,1,0:T(8,128)S(1)} %get-tuple-element.240), kind=kOutput, calls=%fused_computation.15.clone.1 | convolution fusion | flops 171966464 | bytes 17043456 | tf_op jit(solution)/shard_map/while/body/eval_jaxpr/dot_general | solution.py:38
  856.2 25.7 %sqrt_multiply_fusion.2 = f32[256,16384]{0,1:T(8,128)S(1)} fusion(f32[3,256]{1,0:T(4,128)S(1)} %get-tuple-element.277, f32[16384]{0:T(1024)S(1)} %bitcast.107, f32[256]{0:T(256)S(1)} %get-tuple-element.275, f32[1,3,128,128]{3,2,1,0:T(8,128)S(1)} %get-tuple-element.240), kind=kOutput, calls=%fused_computation.15.clone.1 | convolution fusion | flops 171966464 | bytes 17043456 | tf_op jit(solution)/shard_map/while/body/eval_jaxpr/dot_general | solution.py:38
  892.8 25.7 %sqrt_multiply_fusion.2 = f32[256,16384]{0,1:T(8,128)S(1)} fusion(f32[3,256]{1,0:T(4,128)S(1)} %get-tuple-element.277, f32[16384]{0:T(1024)S(1)} %bitcast.107, f32[256]{0:T(256)S(1)} %get-tuple-element.275, f32[1,3,128,128]{3,2,1,0:T(8,128)S(1)} %get-tuple-element.240), kind=kOutput, calls=%fused_computation.15.clone.1 | convolution fusion | flops 171966464 | bytes 17043456 | tf_op jit(solution)/shard_map/while/body/eval_jaxpr/dot_general | solution.py:38
  929.5 25.7 %sqrt_multiply_fusion.2 = f32[256,16384]{0,1:T(8,128)S(1)} fusion(f32[3,256]{1,0:T(4,128)S(1)} %get-tuple-element.277, f32[16384]{0:T(1024)S(1)} %bitcast.107, f32[256]{0:T(256)S(1)} %get-tuple-element.275, f32[1,3,128,128]{3,2,1,0:T(8,128)S(1)} %get-tuple-element.240), kind=kOutput, calls=%fused_computation.15.clone.1 | convolution fusion | flops 171966464 | bytes 17043456 | tf_op jit(solution)/shard_map/while/body/eval_jaxpr/dot_general | solution.py:38
  966.2 25.7 %sqrt_multiply_fusion.2 = f32[256,16384]{0,1:T(8,128)S(1)} fusion(f32[3,256]{1,0:T(4,128)S(1)} %get-tuple-element.277, f32[16384]{0:T(1024)S(1)} %bitcast.107, f32[256]{0:T(256)S(1)} %get-tuple-element.275, f32[1,3,128,128]{3,2,1,0:T(8,128)S(1)} %get-tuple-element.240), kind=kOutput, calls=%fused_computation.15.clone.1 | convolution fusion | flops 171966464 | bytes 17043456 | tf_op jit(solution)/shard_map/while/body/eval_jaxpr/dot_general | solution.py:38
  1001.2 33.2 %psum.23 = f32[3,256]{1,0:T(4,128)S(1)} all-reduce(f32[3,256]{1,0:T(4,128)S(1)} %fusion.41), channel_id=1, replica_groups=mesh['row'=8,'col'=16] {'col'}, use_global_device_ids=true, to_apply=%region_10.11 | all-reduce | flops 768 | bytes 6144 | tf_op jit(solution)/shard_map/psum | solution.py:132
  (138 shorter events, 279.4 us)
Async XLA Ops:
  27.9 140.4 %all-to-all-start = ((f32[3,256,128]{2,0,1:T(4,128)}), f32[3,256,128]{2,0,1:T(4,128)S(1)}, u32[]{:S(2)}, u32[]{:S(2)}) async-start(f32[3,256,128]{2,0,1:T(4,128)} %scatter_fusion), calls=%async_computation | async-start | bytes 1048576 | tf_op jit(solution)/shard_map/all_to_all | solution.py:95
  39.1 374.6 %all-gather.2.cloned.1.call-start = ((), (), s32[]{:S(2)}) async-start(), calls=%async_computation.1 | async-start | bytes 7077888 | tf_op jit(solution)/shard_map/all_gather | solution.py:130
  194.3 23.4 %copy-start = (s32[8,256]{1,0:T(8,128)S(1)}, s32[8,256]{1,0:T(8,128)}, u32[]{:S(2)}) copy-start(s32[8,256]{1,0:T(8,128)} %param.7) | copy-start | bytes 24580
Sparse Core Ops, SparseCore 0:
  217.9 80.3 all-gather.1
